TPU v7x, 256 devices: a whole 4x4x8 slice. The times are simulated.
256 devices in a mesh: group: 16 (over x, y), member: 16 (over z, core).
Axes of the slice: x: 4, y: 4, z: 8, core: 2. Of those that a mesh axis runs over, the one named last changes fastest.
Arguments:
- embeddings: bfloat16 [24576, 4096], P(('group', 'member'))
- cluster_ids: int32 [24576], P(('group', 'member')), may hold values from 0 to 31, as said below
- order_index: int32 [24576], P(('group', 'member')), may hold values from 0 to 24575, each once
Outputs:
- best_similarity: float32 [24576], P(('group', 'member'))
Inputs may be any that keep to these rules, and one draw needn't show every extreme that they name: `cluster_ids`: among the documents of one device, at most 12 have a cluster of any one group index g (cluster // 2 == g), and on every device some group index has exactly 12.
All inputs are finite; a program needn't handle non-finite values.
Results may differ from a plain program's by a relative error of at most 0.0004.
Values may be sent and summed in bfloat16 or wider, within the bound.
A program may use at most 128 MiB of HBM per device.

v0:
```python
import jax
import jax.numpy as jnp
from jax import lax
from jax.sharding import PartitionSpec as P

CL_GROUP = 2


def normalize(embeddings):
    values = embeddings.astype(jnp.float32)
    total = jnp.sum(values * values, axis=1, keepdims=True) + values.shape[1] * 1e-06
    return (values * lax.rsqrt(total)).astype(jnp.bfloat16)


def tile_maxima(rows_left, cluster_left, order_left, rows_right, cluster_right, order_right):
    cosine = lax.dot_general(
        rows_left, rows_right, (((1,), (1,)), ((), ())), preferred_element_type=jnp.float32
    )
    same_cluster = (cluster_left[:, None] == cluster_right[None, :]) & (cluster_left[:, None] >= 0)
    earlier = same_cluster & (order_right[None, :] < order_left[:, None])
    later_pair = same_cluster & (order_left[:, None] < order_right[None, :])
    row_maxima = jnp.max(jnp.where(earlier, cosine, -1.0), axis=1)
    column_max = jnp.max(jnp.where(later_pair, cosine, -1.0), axis=0)
    return (row_maxima, column_max)


def local(embeddings, cluster_ids, order_index):
    groups = lax.axis_size("group")
    row_count = embeddings.shape[0]
    feature_count = embeddings.shape[1]
    capacity = 2 * row_count // groups
    unit_rows = normalize(embeddings)
    target_group = cluster_ids // CL_GROUP
    positions = jnp.arange(row_count, dtype=jnp.int32)
    same_target = target_group[:, None] == target_group[None, :]
    slot_rank = jnp.sum(same_target & (positions[None, :] < positions[:, None]), axis=1)
    slot_index = target_group * capacity + slot_rank
    slot_table = jnp.arange(groups * capacity, dtype=jnp.int32)[:, None] == slot_index[None, :]
    outgoing_rows = jnp.dot(
        slot_table.astype(jnp.bfloat16), unit_rows, preferred_element_type=jnp.float32
    )
    outgoing_rows = outgoing_rows.astype(jnp.bfloat16).reshape(groups, capacity, feature_count)
    outgoing_cluster = (
        jnp.sum(jnp.where(slot_table, cluster_ids[None, :] + 1, 0), axis=1) - 1
    ).reshape(groups, capacity)
    outgoing_order = jnp.sum(jnp.where(slot_table, order_index[None, :], 0), axis=1).reshape(
        groups, capacity
    )
    received, received_cluster, received_order = (
        lax.all_to_all(outgoing_rows, "group", split_axis=0, concat_axis=0, tiled=True),
        lax.all_to_all(outgoing_cluster, "group", split_axis=0, concat_axis=0, tiled=True),
        lax.all_to_all(outgoing_order, "group", split_axis=0, concat_axis=0, tiled=True),
    )
    received = received.reshape(groups * capacity, feature_count)
    received_cluster = received_cluster.reshape(groups * capacity)
    received_order = received_order.reshape(groups * capacity)
    position_count = groups * capacity
    start_value = jnp.full((position_count,), -1.0, dtype=jnp.float32)
    piece_rows = lax.all_gather(received, "member", axis=0, tiled=True)
    piece_cluster = lax.all_gather(received_cluster, "member", axis=0, tiled=True)
    piece_order = lax.all_gather(received_order, "member", axis=0, tiled=True)
    row_maxima, column_max = tile_maxima(
        received, received_cluster, received_order, piece_rows, piece_cluster, piece_order
    )
    best_so_far = jnp.maximum(start_value, row_maxima)
    answered = lax.all_to_all(
        best_so_far.reshape(groups, capacity), "group", split_axis=0, concat_axis=0, tiled=True
    ).reshape(position_count)
    return jnp.sum(jnp.where(slot_table, answered[:, None], 0.0), axis=0)


def solution(mesh):
    placed = (P(("group", "member"), None), P(("group", "member")), P(("group", "member")))
    return jax.shard_map(
        local, mesh=mesh, in_specs=placed, out_specs=P(("group", "member")), check_vma=False
    )
```

profile of v0, /device:TPU:1, one launch (start us, length us, event | category | flops | bytes accessed | tf_op | source)
XLA Modules:
  0.0 225.1 jit_solution(3742905653400254289)
XLA Ops:
  6.5 0.7 broadcast_add_fusion.1
  7.2 0.2 convert_reduce_fusion
  7.4 1.4 fusion
  8.8 2.9 %convolution_convert_fusion = bf16[192,4096]{1,0:T(8,128)(2,1)} fusion(bf16[96,4096]{1,0:T(8,128)(2,1)} %param.3, f32[96]{0:T(128)S(1)} %add_rsqrt_fusion, s32[96]{0:T(128)S(1)} %multiply_add_fusion), kind=kOutput, calls=%fused_computation | convolution fusion | flops 152979456 | bytes 2360064 | tf_op jit(solution)/shard_map/dot_general | solution.py:39
  11.7 2.3 %reshape.77 = bf16[16,12,4096]{2,1,0:T(8,128)(2,1)S(1)} reshape(bf16[192,4096]{1,0:T(8,128)(2,1)} %convolution_convert_fusion) | data formatting | bytes 3145728 | tf_op jit(solution)/shard_map/reshape | solution.py:42
  14.1 34.6 %all_to_all.26 = bf16[16,12,4096]{2,1,0:T(8,128)(2,1)} all-to-all(bf16[16,12,4096]{2,1,0:T(8,128)(2,1)S(1)} %reshape.77), channel_id=1, replica_groups=mesh['group'=16,'member'=16] {'group'}, dimensions={0} | all-to-all | bytes 3145728 | tf_op jit(solution)/shard_map/all_to_all | solution.py:50
  48.7 3.6 %reshape.78 = bf16[192,4096]{1,0:T(8,128)(2,1)} reshape(bf16[16,12,4096]{2,1,0:T(8,128)(2,1)} %all_to_all.26) | data formatting | bytes 3145728 | tf_op jit(solution)/shard_map/reshape | solution.py:54
  52.3 0.0 all-gather.2.cloned.1.call-update
  52.3 0.2 select_reduce_fusion.2
  52.5 0.7 sub.14
  53.2 3.8 %all-to-all-start = ((s32[16,1,12]{2,1,0:T(1,128)}), s32[16,1,12]{2,1,0:T(1,128)S(1)}, u32[]{:S(2)}, u32[]{:S(2)}) async-start(s32[16,1,12]{2,1,0:T(1,128)} %bitcast), calls=%async_computation | async-start | bytes 16384 | tf_op jit(solution)/shard_map/all_to_all | solution.py:51
  57.0 0.7 all_to_all.18
  57.7 5.8 %all-to-all-done = s32[16,1,12]{2,1,0:T(1,128)S(1)} async-done(((s32[16,1,12]{2,1,0:T(1,128)}), s32[16,1,12]{2,1,0:T(1,128)S(1)}, u32[]{:S(2)}, u32[]{:S(2)}) %all-to-all-start) | async-done | bytes 800 | tf_op jit(solution)/shard_map/all_to_all | solution.py:51
  63.4 3.4 %all-to-all-start.1 = ((s32[16,1,12]{2,1,0:T(1,128)}), s32[16,1,12]{2,1,0:T(1,128)S(1)}, u32[]{:S(2)}, u32[]{:S(2)}) async-start(s32[16,1,12]{2,1,0:T(1,128)} %bitcast.2), calls=%async_computation.1 | async-start | bytes 16384 | tf_op jit(solution)/shard_map/all_to_all | solution.py:52
  66.9 0.6 dynamic-slice
  68.1 0.5 broadcast.67
  68.6 0.7 reduce.10
  69.3 0.1 reshape.79
  69.4 3.9 %all-to-all-done.1 = s32[16,1,12]{2,1,0:T(1,128)S(1)} async-done(((s32[16,1,12]{2,1,0:T(1,128)}), s32[16,1,12]{2,1,0:T(1,128)S(1)}, u32[]{:S(2)}, u32[]{:S(2)}) %all-to-all-start.1) | async-done | bytes 800 | tf_op jit(solution)/shard_map/all_to_all | solution.py:52
  73.3 0.7 reduce.9
  73.9 0.1 reshape.82
  74.0 0.3 dynamic-update-slice
  74.3 0.3 dynamic-update-slice.1
  74.6 54.5 %all-reduce.2 = (s32[3072]{0:T(1024)S(1)}, s32[3072]{0:T(1024)S(1)}) all-reduce(s32[3072]{0:T(1024)S(1)} %dynamic-update-slice.1, s32[3072]{0:T(1024)S(1)} %dynamic-update-slice), channel_id=1, replica_groups=mesh['group'=16,'member'=16] {'member'}, use_global_device_ids=true, to_apply=%add.1 | all-reduce | flops 6144 | bytes 49152
  129.1 60.5 %all-gather.2.cloned.1.call-done = bf16[3072,4096]{1,0:T(8,128)(2,1)} async-done(((bf16[192,4096]{1,0:T(8,128)(2,1)}), bf16[3072,4096]{1,0:T(8,128)(2,1)}) %all-gather.2.cloned.1.call-update) | async-done | bytes 25165840 | tf_op jit(solution)/shard_map/all_gather | solution.py:59
  189.6 13.9 %fusion.2 = f32[192]{0:T(256)S(1)} fusion(bf16[192,4096]{1,0:T(8,128)(2,1)} %reshape.78, bf16[3072,4096]{1,0:T(8,128)(2,1)} %all-gather.2.cloned.1.call-done, s32[3072]{0:T(1024)S(1)} %get-tuple-element.7, s32[3072]{0:T(1024)S(1)} %get-tuple-element.8, s32[192]{0:T(256)S(1)} %reshape.82, s32[192]{0:T(256)S(1)} %reshape.79, ...), kind=kOutput, calls=%fused_computation.6 | convolution fusion | flops 4835377152 | bytes 26765760 | tf_op jit(solution)/shard_map/dot_general | solution.py:16
  203.5 0.1 max_broadcast_in_dim.15
  203.6 12.8 %all_to_all.27 = f32[16,1,12]{2,1,0:T(1,128)S(1)} all-to-all(f32[16,1,12]{2,1,0:T(1,128)S(1)} %bitcast.6), channel_id=1, replica_groups=mesh['group'=16,'member'=16] {'group'}, dimensions={0} | all-to-all | bytes 1536 | tf_op jit(solution)/shard_map/all_to_all | solution.py:66
  216.4 0.5 broadcast.69
  216.9 0.7 reduce.11
  217.6 0.1 broadcast_in_dim.55
  217.7 0.6 select_reduce_fusion
  (12 shorter events, 0.0 us)
Async XLA Ops:
  6.5 183.1 %all-gather.2.cloned.1.call-start = ((), (), s32[]{:S(2)}) async-start(), calls=%async_computation.4 | async-start | bytes 26738688 | tf_op jit(solution)/shard_map/all_gather | solution.py:59
  48.7 3.6 %copy-start = (s32[96]{0:T(128)S(1)}, s32[96]{0:T(128)}, u32[]{:S(2)}) copy-start(s32[96]{0:T(128)} %param.5) | copy-start | bytes 1156
  48.7 18.2 %copy-start.1 = (u32[256]{0:T(256)S(1)}, u32[256]{0:T(256)}, u32[]{:S(2)}) copy-start(u32[256]{0:T(256)} %constant.35) | copy-start | bytes 3076
  53.2 10.2 %all-to-all-start = ((s32[16,1,12]{2,1,0:T(1,128)}), s32[16,1,12]{2,1,0:T(1,128)S(1)}, u32[]{:S(2)}, u32[]{:S(2)}) async-start(s32[16,1,12]{2,1,0:T(1,128)} %bitcast), calls=%async_computation | async-start | bytes 16384 | tf_op jit(solution)/shard_map/all_to_all | solution.py:51
  63.4 9.8 %all-to-all-start.1 = ((s32[16,1,12]{2,1,0:T(1,128)}), s32[16,1,12]{2,1,0:T(1,128)S(1)}, u32[]{:S(2)}, u32[]{:S(2)}) async-start(s32[16,1,12]{2,1,0:T(1,128)} %bitcast.2), calls=%async_computation.1 | async-start | bytes 16384 | tf_op jit(solution)/shard_map/all_to_all | solution.py:52
Sparse Core Ops, SparseCore 0:
  52.5 137.1 all-gather.1
where the time goes:
time: 226 us; the launch traced here: 225 us
  blocking collectives  102 us (45%)
  waiting for transfers between devices  70.1 us (31%)
  matrix products  16.8 us (7%)
  between operations  14.2 us (6%)
  local copies, waits for them, and re-layouts  9.78 us (4%)
  starting transfers between devices  7.23 us (3%)
  other arithmetic  5.04 us (2%)
    all_gather x1, waiting for transfers between devices, local(): piece_rows = lax.all_gather(received, 'member', axis=0, tiled=True)  60.5 us
    unnamed x1, blocking collectives  54.5 us
    all_to_all x1, blocking collectives, local(): lax.all_to_all(outgoing_rows, 'group', split_axis=0, concat_axis=0, tiled...  34.6 us
    dot_general x1, matrix products, tile_maxima(): lax.dot_general(rows_left, rows_right, (((1,), (1,)), ((), ())), preferre...  13.9 us
    all_to_all x1, blocking collectives, local(): lax.all_to_all(best_so_far.reshape(groups, capacity), 'group', split_axis...  12.8 us
    all_to_all x1, waiting for transfers between devices, local(): lax.all_to_all(outgoing_cluster, 'group', split_axis=0, concat_axis=0, ti...  5.76 us
  transfers between devices with their start and end apart: 3, of which 3 were waited for; matrix products, arithmetic and copies ran while one was open for 2% of the time, Pallas kernels for 0%

commit v1 on v0

v1 whole, which is shorter than its diff:
```python
import functools

import jax
import jax.numpy as jnp
from jax import lax
from jax.experimental import pallas as pl
from jax.experimental.pallas import tpu as pltpu
from jax.sharding import PartitionSpec as P

MESH = pl.DeviceIdType.MESH

NX, NY, NZ = 4, 4, 8
DOCS = 96
CAP = 12
CHUNK = 2 * CAP
SLOTS = NZ * CHUNK
D = 4096
META = 128
W = D + META

XM, XP, X2, OWN, YM, YP, Y2 = range(7)
ORDER = (0, 1, 7, 2, 6, 3, 5, 4)


def nt_dot(a, b, **kw):
    return lax.dot_general(
        a, b, (((1,), (1,)), ((), ())), preferred_element_type=jnp.float32, **kw
    )


def kernel(
    emb_ref,
    ids_ref,
    ord_ref,
    out_ref,
    units,
    mrows,
    outb,
    buf,
    best,
    part,
    ans,
    fin,
    sib_send,
    sib_recv,
    z_send,
    send,
    recv,
    p_send,
    p_recv,
    a_send,
    a_recv,
):
    gi = lax.axis_index("group")
    mi = lax.axis_index("member")
    x, y = gi // NY, lax.rem(gi, NY)
    z, c = mi // 2, lax.rem(mi, 2)

    def at_x(step):
        return (lax.rem(x + step + NX, NX) * NY + y, mi)

    def at_y(step):
        return (x * NY + lax.rem(y + step + NY, NY), mi)

    def at_z(step):
        return (gi, lax.rem(z + step + NZ, NZ) * 2 + c)

    sibling = (gi, z * 2 + 1 - c)

    peers = [sibling, at_x(1), at_x(-1), at_y(1), at_y(-1), at_y(2)]
    peers += [at_z(s) for s in range(1, NZ)]
    barrier = pltpu.get_barrier_semaphore()
    for peer in peers:
        pl.semaphore_signal(barrier, inc=1, device_id=peer, device_id_type=MESH)

    @pl.loop(0, DOCS // 16)
    def _(i):
        rows = pl.ds(pl.multiple_of(i * 16, 16), 16)
        values = emb_ref[rows, :].astype(jnp.float32)
        total = jnp.sum(values * values, axis=1, keepdims=True) + D * 1e-06
        units[0, rows, :] = (values * lax.rsqrt(total)).astype(jnp.bfloat16)

    ids = ids_ref[...]
    order = ord_ref[...]
    target = ids // 2
    hit = lax.broadcasted_iota(jnp.int32, (16, DOCS), 0) == target
    hit_f = hit.astype(jnp.float32)
    tri = lax.broadcasted_iota(jnp.int32, (DOCS, DOCS), 0) < lax.broadcasted_iota(
        jnp.int32, (DOCS, DOCS), 1
    )
    count = jnp.dot(
        hit_f.astype(jnp.bfloat16), tri.astype(jnp.bfloat16), preferred_element_type=jnp.float32
    )
    rank = jnp.sum(hit_f * count, axis=0, keepdims=True).astype(jnp.int32)
    offset = lax.rem(target // 2 - z + NZ, NZ)
    core = lax.rem(target, 2)
    inner = c * CAP + rank
    slot = offset * CHUNK + inner
    to_core0 = jnp.where(core == 0, slot, -1).astype(jnp.float32)
    to_core1 = jnp.where(core == 1, slot, -1).astype(jnp.float32)
    high = order // 256
    low = order - high * 256
    row_id = lax.broadcasted_iota(jnp.int32, (8, DOCS), 0)
    packed = jnp.where(row_id == 0, to_core0, 0.0)
    packed = jnp.where(row_id == 1, to_core1, packed)
    packed = jnp.where(row_id == 2, (ids + 1).astype(jnp.float32), packed)
    packed = jnp.where(row_id == 3, high.astype(jnp.float32), packed)
    packed = jnp.where(row_id == 4, low.astype(jnp.float32), packed)
    mrows[0, :, :DOCS] = packed
    mrows[0, :, DOCS:] = jnp.zeros((8, 128 - DOCS), jnp.float32)

    pl.semaphore_wait(barrier, len(peers))

    waits = []

    def push(src, dst, ssem, rsem, device):
        copy = pltpu.make_async_remote_copy(
            src_ref=src, dst_ref=dst, send_sem=ssem, recv_sem=rsem,
            device_id=device, device_id_type=MESH,
        )
        copy.start()
        waits.append(copy)
        return copy

    meta_copy = push(mrows.at[0], mrows.at[1], sib_send.at[0], sib_recv.at[0], sibling)
    unit_copy = push(units.at[0], units.at[1], sib_send.at[1], sib_recv.at[1], sibling)

    slot_iota = lax.broadcasted_iota(jnp.int32, (SLOTS, DOCS), 0).astype(jnp.float32)

    def table_of(which):
        rows = mrows[which]
        mine = jnp.where(c == 0, rows[0:1, :DOCS], rows[1:2, :DOCS])
        table = (slot_iota == mine).astype(jnp.bfloat16)
        lanes = lax.broadcasted_iota(jnp.int32, (META, DOCS), 0)
        cols = jnp.where(lanes == 0, rows[2:3, :DOCS], 0.0)
        cols = jnp.where(lanes == 1, rows[3:4, :DOCS], cols)
        cols = jnp.where(lanes == 2, rows[4:5, :DOCS], cols)
        return table, nt_dot(table, cols.astype(jnp.bfloat16))

    table_a, meta_a = table_of(0)
    meta_copy.wait_recv()
    table_b, meta_b = table_of(1)
    unit_copy.wait_recv()

    def place(values, columns):
        values = values.reshape(NZ, CHUNK, values.shape[-1]).astype(jnp.bfloat16)
        buf[OWN, 0, :, columns] = values[0]
        outb[:, :, columns] = values[1:]

    place(meta_a + meta_b, pl.ds(D, META))

    @pl.loop(0, D // 512)
    def _(i):
        columns = pl.ds(pl.multiple_of(i * 512, 512), 512)
        rows = jnp.dot(table_a, units[0, :, columns], preferred_element_type=jnp.float32)
        rows += jnp.dot(table_b, units[1, :, columns], preferred_element_type=jnp.float32)
        place(rows, columns)

    own_copies = {}
    for k in ORDER[1:]:
        own_copies[k] = push(outb.at[k - 1], buf.at[OWN, k], z_send.at[k], recv.at[OWN, k], at_z(k))

    arrive = {}

    def forward(src, entry, k, device):
        arrive[entry, k] = push(
            buf.at[src, k], buf.at[entry, k], send.at[entry, k], recv.at[entry, k], device
        )

    done = set()

    def arrived(entry, k):
        if (entry, k) not in done:
            done.add((entry, k))
            arrive[entry, k].wait_recv()

    def relay(i):
        k = ORDER[i]
        if i % 2 == 0:
            arrived(XM, k)
            forward(XM, X2, k, at_x(1))
            arrived(YM, k)
            forward(YM, Y2, k, at_y(1))
        else:
            arrived(XP, k)
            forward(XP, X2, k, at_x(-1))
            arrived(YP, k)
            forward(YP, Y2, k, at_y(-1))

    for i, k in enumerate(ORDER):
        if k:
            own_copies[k].wait_recv()
        forward(OWN, XM, k, at_x(1))
        forward(OWN, XP, k, at_x(-1))
        forward(OWN, YM, k, at_y(1))
        forward(OWN, YP, k, at_y(-1))
        if i:
            relay(i - 1)
    relay(NZ - 1)
    for k in ORDER:
        for entry in (XM, XP, YM, YP, X2, Y2):
            arrived(entry, k)

    best[...] = jnp.full(best.shape, -1.0, jnp.float32)
    pick_row = lax.broadcasted_iota(jnp.int32, (8, META), 0)
    pick_lane = lax.broadcasted_iota(jnp.int32, (8, META), 1)
    pick = jnp.where((pick_row == 0) & (pick_lane == 0), 1.0, 0.0)
    pick = jnp.where((pick_row == 1) & (pick_lane == 1), 256.0, pick)
    pick = jnp.where((pick_row == 1) & (pick_lane == 2), 1.0, pick).astype(jnp.bfloat16)

    @pl.loop(0, 16)
    def _(i):
        r, col = i // 4, OWN + lax.rem(i, 4)
        rows = buf[r, :, :, :D].reshape(SLOTS, D)
        columns = buf[col, :, :, :D].reshape(SLOTS, D)
        cosine = nt_dot(rows, columns)
        rmeta = buf[r, :, :, D:].reshape(SLOTS, META).astype(jnp.float32)
        cmeta = nt_dot(pick, buf[col, :, :, D:].reshape(SLOTS, META))
        rank_r = rmeta[:, 1:2] * 256.0 + rmeta[:, 2:3]
        keep = (rmeta[:, 0:1] == cmeta[0:1, :]) & (rank_r < cmeta[1:2, :])
        masked = jnp.where(keep, cosine, -1.0).reshape(SLOTS // 8, 8, SLOTS)
        j = col - OWN
        best[j, :, :SLOTS] = jnp.maximum(best[j, :, :SLOTS], jnp.max(masked, axis=0))

    p_copies = []
    for n, (entry, step) in enumerate(((YM, -1), (YP, 1), (Y2, 2))):
        p_copies.append(
            push(best.at[entry - OWN], part.at[n], p_send.at[n], p_recv.at[n], at_y(step))
        )
    for copy in p_copies:
        copy.wait_recv()
    total = jnp.maximum(
        jnp.maximum(best[0], part[0]), jnp.maximum(part[1], part[2])
    )
    total = jnp.max(total, axis=0, keepdims=True)
    ans[0] = jnp.broadcast_to(total, (8, 256))
    a_copies = []
    for k in range(1, NZ):
        a_copies.append(push(ans.at[0], ans.at[k], a_send.at[k], a_recv.at[k], at_z(-k)))
    for copy in a_copies:
        copy.wait_recv()
    fin[0] = jnp.zeros((8, 128), jnp.float32)
    for k in range(NZ):
        fin[0, k : k + 1, :CHUNK] = ans[k, 0:1, k * CHUNK : (k + 1) * CHUNK]
    fin_copy = push(fin.at[0], fin.at[1], sib_send.at[2], sib_recv.at[2], sibling)
    spot = (lax.broadcasted_iota(jnp.int32, (128, DOCS), 0) == inner).astype(jnp.float32)
    offs = lax.broadcasted_iota(jnp.int32, (8, DOCS), 0) == offset
    fin_copy.wait_recv()
    picked = jnp.zeros((8, DOCS), jnp.float32)
    for n in range(2):
        values = jnp.dot(
            fin[n], spot, preferred_element_type=jnp.float32, precision=lax.Precision.HIGHEST
        )
        at_core = jnp.where(core == (c if n == 0 else 1 - c), 1, 0)
        picked += jnp.where(offs & (at_core == 1), values, 0.0)
    out_ref[...] = jnp.sum(picked, axis=0, keepdims=True)
    for copy in waits:
        copy.wait_send()


def local(embeddings, cluster_ids, order_index):
    dma = pltpu.SemaphoreType.DMA
    vmem = pl.BlockSpec(memory_space=pltpu.VMEM)
    result = pl.pallas_call(
        kernel,
        out_shape=jax.ShapeDtypeStruct((1, DOCS), jnp.float32),
        in_specs=[vmem] * 3,
        out_specs=vmem,
        scratch_shapes=[
            pltpu.VMEM((2, DOCS, D), jnp.bfloat16),
            pltpu.VMEM((2, 8, 128), jnp.float32),
            pltpu.VMEM((NZ - 1, CHUNK, W), jnp.bfloat16),
            pltpu.VMEM((7, NZ, CHUNK, W), jnp.bfloat16),
            pltpu.VMEM((4, 8, 256), jnp.float32),
            pltpu.VMEM((3, 8, 256), jnp.float32),
            pltpu.VMEM((NZ, 8, 256), jnp.float32),
            pltpu.VMEM((2, 8, 128), jnp.float32),
            dma((3,)),
            dma((3,)),
            dma((NZ,)),
            dma((7, NZ)),
            dma((7, NZ)),
            dma((3,)),
            dma((3,)),
            dma((NZ,)),
            dma((NZ,)),
        ],
        compiler_params=pltpu.CompilerParams(
            collective_id=0, has_side_effects=True, vmem_limit_bytes=48 * 1024 * 1024
        ),
    )(embeddings, cluster_ids.reshape(1, DOCS), order_index.reshape(1, DOCS))
    return result.reshape(DOCS)


def solution(mesh):
    placed = (P(("group", "member"), None), P(("group", "member")), P(("group", "member")))
    return jax.shard_map(
        local, mesh=mesh, in_specs=placed, out_specs=P(("group", "member")), check_vma=False
    )
```

time: 226 us -> 97.4 us (0.43)
  blocking collectives: 102 us -> 0 us
  Pallas kernels: 0 us -> 94.9 us
  waiting for transfers between devices: 70.1 us -> 0 us
  matrix products: 16.8 us -> 0 us
  between operations: 14.2 us -> 0.01 us
  local copies, waits for them, and re-layouts: 9.78 us -> 2.32 us
  starting transfers between devices: 7.23 us -> 0 us
  other arithmetic: 5.04 us -> 0 us
    pallas_call x0 -> x1, Pallas kernels: none -> 94.9 us  [local(): pl.pallas_call(kernel, out_shape=jax.ShapeDtypeStruct((1, DOCS), jnp.floa...]
    all_gather x1 -> x0, waiting for transfers between devices: 60.5 us -> none  [local(): piece_rows = lax.all_gather(received, 'member', axis=0, tiled=True)]
    unnamed x1 -> x0, blocking collectives: 54.5 us -> none
    all_to_all x2 -> x0, blocking collectives: 47.4 us -> none  [the longest x1 34.6 us: local(): lax.all_to_all(outgoing_rows, 'group', split_axis=0, concat_axis=0, tiled...]
    dot_general x2 -> x0, matrix products: 16.8 us -> none  [the longest x1 13.9 us: tile_maxima(): lax.dot_general(rows_left, rows_right, (((1,), (1,)), ((), ())), preferre...]
    all_to_all x2 -> x0, waiting for transfers between devices: 9.61 us -> none  [the longest x1 5.76 us: local(): lax.all_to_all(outgoing_cluster, 'group', split_axis=0, concat_axis=0, ti...]
    all_to_all x2 -> x0, starting transfers between devices: 7.23 us -> none  [the longest x1 3.8 us: local(): lax.all_to_all(outgoing_cluster, 'group', split_axis=0, concat_axis=0, ti...]
    reshape x3 -> x0, local copies, waits for them, and re-layouts: 6 us -> none  [the longest x1 3.6 us: local(): received = received.reshape(groups * capacity, feature_count)]
  transfers between devices with their start and end apart: 3 -> 0, of which waited for: 3 -> 0; matrix products, arithmetic and copies ran while one was open for 2% -> 0% of each run, Pallas kernels for 0% -> 0%
where the time goes in v1:
time: 97.4 us; the launch traced here: 97.2 us
  Pallas kernels  94.9 us (97%)
  local copies, waits for them, and re-layouts  2.32 us (2%)
    pallas_call x1, Pallas kernels, local(): pl.pallas_call(kernel, out_shape=jax.ShapeDtypeStruct((1, DOCS), jnp.floa...  94.9 us
    unnamed x7, local copies, waits for them, and re-layouts  2.32 us

profile of v1, /device:TPU:1, one launch (start us, length us, event | category | flops | bytes accessed | tf_op | source)
XLA Modules:
  0.0 97.2 jit_solution(2140488669991421028)
XLA Ops:
  0.0 0.0 copy-start.1
  0.0 0.0 copy-start.2
  0.0 0.7 copy-done.1
  0.7 0.0 copy-done.2
  0.7 0.0 copy-start
  0.7 1.1 %copy-done = bf16[96,4096]{1,0:T(8,128)(2,1)S(1)} copy-done((bf16[96,4096]{1,0:T(8,128)(2,1)S(1)}, bf16[96,4096]{1,0:T(8,128)(2,1)}, u32[]{:S(2)}) %copy-start) | copy-done | bytes 786456
  1.8 94.9 %shard_map.37 = f32[1,96]{1,0:T(1,128)S(1)} custom-call(bf16[96,4096]{1,0:T(8,128)(2,1)S(1)} %copy-done, s32[1,96]{1,0:T(1,128)S(1)} %bitcast.3, s32[1,96]{1,0:T(1,128)S(1)} %bitcast.4), custom_call_target="tpu_custom_call" | custom-call | tf_op jit(solution)/shard_map/pallas_call | solution.py:264
  96.7 0.5 copy.5
Async XLA Ops:
  0.0 0.7 copy-start.1
  0.0 0.7 copy-start.2
  0.7 1.1 %copy-start = (bf16[96,4096]{1,0:T(8,128)(2,1)S(1)}, bf16[96,4096]{1,0:T(8,128)(2,1)}, u32[]{:S(2)}) copy-start(bf16[96,4096]{1,0:T(8,128)(2,1)} %emb_ref.1) | copy-start | bytes 2359300

commit v2 on v1

v2 whole, which is shorter than its diff:
```python
import jax
import jax.numpy as jnp
from jax import lax
from jax.experimental import pallas as pl
from jax.experimental.pallas import tpu as pltpu
from jax.sharding import PartitionSpec as P

MESH = pl.DeviceIdType.MESH

NX, NY, NZ = 4, 4, 8
DOCS = 96
CAP = 12
CHUNK = 2 * CAP
SLOTS = NZ * CHUNK
D = 4096
META = 128
WIDTHS = (512,) * 8
STARTS = tuple(sum(WIDTHS[:p]) for p in range(len(WIDTHS)))
PARTS = len(WIDTHS)

OWN, XY, X1, X2, Y1, Y2 = range(6)
BLOCKS = 6
RETURNS = (X1, Y1, XY, X2, Y2)


def nt_dot(a, b):
    return lax.dot_general(
        a, b, (((1,), (1,)), ((), ())), preferred_element_type=jnp.float32
    )


def kernel(*refs):
    emb_hbm, ids_hbm, ord_hbm, out_ref, emb, ids_ref, ord_ref = refs[:7]
    downs, mrows, best, part, ans, fin, acc_own, acc_xy, units = refs[7:16]
    outb = refs[16 : 16 + PARTS]
    buf = refs[16 + PARTS : 16 + 2 * PARTS]
    (
        in_sem, sib_send, sib_recv, z_send, z_recv, send, recv, p_send, p_recv, a_send, a_recv,
    ) = refs[16 + 2 * PARTS :]

    gi = lax.axis_index("group")
    mi = lax.axis_index("member")
    x, y = gi // NY, lax.rem(gi, NY)
    z, c = mi // 2, lax.rem(mi, 2)
    sign = 1 - 2 * c

    def at(dx, dy):
        return (
            lax.rem(x + sign * dx + NX, NX) * NY + lax.rem(y + sign * dy + NY, NY),
            mi,
        )

    def at_z(step):
        return (gi, lax.rem(z + step + NZ, NZ) * 2 + c)

    sibling = (gi, z * 2 + 1 - c)
    back = {X1: at(-1, 0), Y1: at(0, -1), XY: at(-1, -1), X2: at(-2, 0), Y2: at(0, -2)}

    loads = [
        pltpu.make_async_copy(ids_hbm, ids_ref, in_sem.at[0]),
        pltpu.make_async_copy(ord_hbm, ord_ref, in_sem.at[1]),
        pltpu.make_async_copy(emb_hbm, emb, in_sem.at[2]),
    ]
    for load in loads:
        load.start()

    peers = [sibling, at(1, 0), at(0, 1), at(1, 1), at(-1, 0), at(0, -1), at(-1, -1)]
    peers += [at(2, 0), at(0, 2)] + [at_z(s) for s in range(1, NZ)]
    barrier = pltpu.get_barrier_semaphore()
    for peer in peers:
        pl.semaphore_signal(barrier, inc=1, device_id=peer, device_id_type=MESH)

    loads[0].wait()
    loads[1].wait()
    ids = ids_ref[...]
    order = ord_ref[...]
    target = ids // 2
    hit = lax.broadcasted_iota(jnp.int32, (16, DOCS), 0) == target
    hit_f = hit.astype(jnp.float32)
    tri = lax.broadcasted_iota(jnp.int32, (DOCS, DOCS), 0) < lax.broadcasted_iota(
        jnp.int32, (DOCS, DOCS), 1
    )
    count = jnp.dot(
        hit_f.astype(jnp.bfloat16), tri.astype(jnp.bfloat16), preferred_element_type=jnp.float32
    )
    rank = jnp.sum(hit_f * count, axis=0, keepdims=True).astype(jnp.int32)
    offset = lax.rem(target // 2 - z + NZ, NZ)
    core = lax.rem(target, 2)
    inner = c * CAP + rank
    slot = offset * CHUNK + inner
    to_core0 = jnp.where(core == 0, slot, -1).astype(jnp.float32)
    to_core1 = jnp.where(core == 1, slot, -1).astype(jnp.float32)
    high = order // 256
    low = order - high * 256
    row_id = lax.broadcasted_iota(jnp.int32, (8, DOCS), 0)
    packed = jnp.where(row_id == 0, to_core0, 0.0)
    packed = jnp.where(row_id == 1, to_core1, packed)
    packed = jnp.where(row_id == 2, (ids + 1).astype(jnp.float32), packed)
    packed = jnp.where(row_id == 3, high.astype(jnp.float32), packed)
    packed = jnp.where(row_id == 4, low.astype(jnp.float32), packed)
    mrows[0, :, :DOCS] = packed
    mrows[0, :, DOCS:] = jnp.zeros((8, 128 - DOCS), jnp.float32)

    loads[2].wait()

    @pl.loop(0, DOCS // 16)
    def _(i):
        rows = pl.ds(pl.multiple_of(i * 16, 16), 16)
        values = emb[rows, :].astype(jnp.float32)
        total = jnp.sum(values * values, axis=1, keepdims=True) + D * 1e-06
        units[0, rows, :] = (values * lax.rsqrt(total)).astype(jnp.bfloat16)

    pl.semaphore_wait(barrier, len(peers))

    sent = []

    def push(src, dst, ssem, rsem, device):
        copy = pltpu.make_async_remote_copy(
            src_ref=src, dst_ref=dst, send_sem=ssem, recv_sem=rsem,
            device_id=device, device_id_type=MESH,
        )
        copy.start()
        sent.append(copy)
        return copy

    meta_copy = push(
        mrows.at[0], mrows.at[1], sib_send.at[PARTS], sib_recv.at[PARTS], sibling
    )
    unit_copies = []
    for p in range(PARTS):
        columns = pl.ds(STARTS[p], WIDTHS[p])
        unit_copies.append(
            push(
                units.at[0, :, columns], units.at[1, :, columns],
                sib_send.at[p], sib_recv.at[p], sibling,
            )
        )

    slot_iota = lax.broadcasted_iota(jnp.int32, (SLOTS, DOCS), 0).astype(jnp.float32)

    def table_of(which):
        rows = mrows[which]
        mine = jnp.where(c == 0, rows[0:1, :DOCS], rows[1:2, :DOCS])
        table = (slot_iota == mine).astype(jnp.bfloat16)
        lanes = lax.broadcasted_iota(jnp.int32, (META, DOCS), 0)
        cols = jnp.where(lanes == 0, rows[2:3, :DOCS], 0.0)
        cols = jnp.where(lanes == 1, rows[3:4, :DOCS], cols)
        cols = jnp.where(lanes == 2, rows[4:5, :DOCS], cols)
        return table, nt_dot(table, cols.astype(jnp.bfloat16))

    table_a, meta_a = table_of(0)
    meta_copy.wait_recv()
    table_b, meta_b = table_of(1)

    def place(p, values, start):
        width = values.shape[-1]
        values = values.reshape(NZ, CHUNK, width).astype(jnp.bfloat16)
        buf[p][OWN, 0, :, start : start + width] = values[0]
        outb[p][:, :, start : start + width] = values[1:]

    z_copies = {}
    place(0, meta_a + meta_b, WIDTHS[0])
    for p in range(PARTS):
        unit_copies[p].wait_recv()
        columns = pl.ds(STARTS[p], WIDTHS[p])
        rows = jnp.dot(table_a, units[0, :, columns], preferred_element_type=jnp.float32)
        rows += jnp.dot(table_b, units[1, :, columns], preferred_element_type=jnp.float32)
        place(p, rows, 0)
        for k in (1, 7, 2, 6, 3, 5, 4):
            z_copies[p, k] = push(
                outb[p].at[k - 1], buf[p].at[OWN, k], z_send.at[p, k], z_recv.at[p, k], at_z(k)
            )

    copies = {}

    def forward(src, dst, p, device):
        copies[dst, p] = push(
            buf[p].at[src], buf[p].at[dst], send.at[dst, p], recv.at[dst, p], device
        )

    done = set()

    def arrived(block, p):
        if (block, p) not in done:
            done.add((block, p))
            copies[block, p].wait_recv()

    def relay(p):
        arrived(X1, p)
        forward(X1, X2, p, at(1, 0))
        if p % 2 == 0:
            forward(X1, XY, p, at(0, 1))
        arrived(Y1, p)
        forward(Y1, Y2, p, at(0, 1))
        if p % 2 == 1:
            forward(Y1, XY, p, at(1, 0))

    def multiply(p):
        for block in (XY, X2, Y2):
            arrived(block, p)
        w = WIDTHS[p]
        rows = buf[p][OWN, :, :, :w].reshape(SLOTS, w)
        for block in range(BLOCKS):
            acc_own[block] += nt_dot(buf[p][block, :, :, :w].reshape(SLOTS, w), rows)
        for b in range(2):
            columns = buf[p][Y1 + b, :, :, :w].reshape(SLOTS, w)
            for a in range(2):
                acc_xy[a, b] += nt_dot(buf[p][X1 + a, :, :, :w].reshape(SLOTS, w), columns)

    pick_row = lax.broadcasted_iota(jnp.int32, (8, META), 0)
    pick_lane = lax.broadcasted_iota(jnp.int32, (8, META), 1)
    pick = jnp.where((pick_row == 0) & (pick_lane == 0), 1.0, 0.0)
    pick = jnp.where((pick_row == 1) & (pick_lane == 1), 256.0, pick)
    pick = jnp.where((pick_row == 1) & (pick_lane == 2), 1.0, pick).astype(jnp.bfloat16)

    def meta_of(block):
        return buf[0][block, :, :, WIDTHS[0] :].reshape(SLOTS, META)

    def meta_down(block):
        values = meta_of(block).astype(jnp.float32)
        return values[:, 0:1], values[:, 1:2] * 256.0 + values[:, 2:3]

    def meta_across(block):
        values = nt_dot(pick, meta_of(block))
        return values[0:1, :], values[1:2, :]

    def start_sums():
        for block in (XY, X2, Y2):
            arrived(block, 0)
        across = {b: meta_across(b)[0] for b in (OWN, Y1, Y2)}
        for block in range(BLOCKS):
            down = meta_down(block)[0]
            acc_own[block] = jnp.where(down == across[OWN], 0.0, -4.0)
            if block in (X1, X2):
                for b in range(2):
                    acc_xy[block - X1, b] = jnp.where(down == across[Y1 + b], 0.0, -4.0)
        downs[...] = jnp.full(downs.shape, -1.0, jnp.float32)

    for p in range(PARTS):
        for k in (1, 7, 2, 6, 3, 5, 4):
            z_copies[p, k].wait_recv()
        forward(OWN, X1, p, at(1, 0))
        forward(OWN, Y1, p, at(0, 1))
        if p >= 1:
            relay(p - 1)
        if p == 2:
            start_sums()
        if p >= 2:
            multiply(p - 2)
    relay(PARTS - 1)
    multiply(PARTS - 2)
    multiply(PARTS - 1)

    def over_rows(sums, down, across):
        kept = jnp.where(down < across, sums, -1.0)
        return jnp.max(kept.reshape(SLOTS // 8, 8, SLOTS), axis=0)

    def over_columns(sums, down, across):
        return jnp.where(across < down, sums, -1.0)

    across = {b: meta_across(b)[1] for b in (OWN, Y1, Y2)}
    down = {b: meta_down(b)[1] for b in range(BLOCKS)}
    lanes = {b: None for b in range(BLOCKS)}
    rows = {b: None for b in range(BLOCKS)}

    def merge(table, key, value):
        table[key] = value if table[key] is None else jnp.maximum(table[key], value)

    for a in range(2):
        for b in range(2):
            sums = acc_xy[a, b]
            merge(rows, X1 + a, over_columns(sums, down[X1 + a], across[Y1 + b]))
            if (a, b) != (1, 1):
                merge(lanes, Y1 + b, over_rows(sums, down[X1 + a], across[Y1 + b]))
    for block in range(BLOCKS):
        sums = acc_own[block]
        merge(lanes, OWN, over_rows(sums, down[block], across[OWN]))
        if block in (XY, X1, Y1):
            merge(rows, block, over_columns(sums, down[block], across[OWN]))
    for n, block in enumerate((XY, X1, X2, Y1)):
        downs[n, :, :SLOTS] = rows[block]
        narrow = jnp.maximum(downs[n, :, :128], downs[n, :, 128:])
        turned = jnp.max(narrow.T, axis=0, keepdims=True)
        merge(lanes, block, jnp.broadcast_to(turned, (8, SLOTS)))
    for block in range(BLOCKS):
        best[block, :, :SLOTS] = lanes[block]

    p_copies = []
    for n, block in enumerate(RETURNS):
        p_copies.append(push(best.at[block], part.at[n], p_send.at[n], p_recv.at[n], back[block]))
    total = best[OWN]
    for n in range(len(RETURNS)):
        p_copies[n].wait_recv()
        total = jnp.maximum(total, part[n])
    total = jnp.max(total, axis=0, keepdims=True)
    ans[0] = jnp.broadcast_to(total, (8, 256))
    a_copies = []
    for k in range(1, NZ):
        a_copies.append(push(ans.at[0], ans.at[k], a_send.at[k], a_recv.at[k], at_z(-k)))
    for copy in a_copies:
        copy.wait_recv()
    fin[0] = jnp.zeros((8, 128), jnp.float32)
    for k in range(NZ):
        fin[0, k : k + 1, :CHUNK] = ans[k, 0:1, k * CHUNK : (k + 1) * CHUNK]
    fin_copy = push(
        fin.at[0], fin.at[1], sib_send.at[PARTS + 1], sib_recv.at[PARTS + 1], sibling
    )
    spot = (lax.broadcasted_iota(jnp.int32, (128, DOCS), 0) == inner).astype(jnp.float32)
    offs = lax.broadcasted_iota(jnp.int32, (8, DOCS), 0) == offset
    fin_copy.wait_recv()
    picked = jnp.zeros((8, DOCS), jnp.float32)
    for n in range(2):
        values = jnp.dot(
            fin[n], spot, preferred_element_type=jnp.float32, precision=lax.Precision.HIGHEST
        )
        at_core = jnp.where(core == (c if n == 0 else 1 - c), 1, 0)
        picked += jnp.where(offs & (at_core == 1), values, 0.0)
    out_ref[...] = jnp.sum(picked, axis=0, keepdims=True)
    for copy in sent:
        copy.wait_send()


def local(embeddings, cluster_ids, order_index):
    dma = pltpu.SemaphoreType.DMA
    f32, bf16 = jnp.float32, jnp.bfloat16
    widths = [w + (META if p == 0 else 0) for p, w in enumerate(WIDTHS)]
    result = pl.pallas_call(
        kernel,
        out_shape=jax.ShapeDtypeStruct((1, DOCS), jnp.float32),
        in_specs=[pl.BlockSpec(memory_space=pltpu.HBM)] * 3,
        out_specs=pl.BlockSpec(memory_space=pltpu.VMEM),
        scratch_shapes=[
            pltpu.VMEM((DOCS, D), bf16),
            pltpu.VMEM((1, DOCS), jnp.int32),
            pltpu.VMEM((1, DOCS), jnp.int32),
            pltpu.VMEM((4, SLOTS, 256), f32),
            pltpu.VMEM((2, 8, 128), f32),
            pltpu.VMEM((BLOCKS, 8, 256), f32),
            pltpu.VMEM((len(RETURNS), 8, 256), f32),
            pltpu.VMEM((NZ, 8, 256), f32),
            pltpu.VMEM((2, 8, 128), f32),
            pltpu.VMEM((BLOCKS, SLOTS, SLOTS), f32),
            pltpu.VMEM((2, 2, SLOTS, SLOTS), f32),
            pltpu.VMEM((2, DOCS, D), bf16),
        ]
        + [pltpu.VMEM((NZ - 1, CHUNK, w), bf16) for w in widths]
        + [pltpu.VMEM((BLOCKS, NZ, CHUNK, w), bf16) for w in widths]
        + [
            dma((3,)),
            dma((PARTS + 2,)),
            dma((PARTS + 2,)),
            dma((PARTS, NZ)),
            dma((PARTS, NZ)),
            dma((BLOCKS, PARTS)),
            dma((BLOCKS, PARTS)),
            dma((len(RETURNS),)),
            dma((len(RETURNS),)),
            dma((NZ,)),
            dma((NZ,)),
        ],
        compiler_params=pltpu.CompilerParams(
            collective_id=0, has_side_effects=True, vmem_limit_bytes=48 * 1024 * 1024
        ),
    )(embeddings, cluster_ids.reshape(1, DOCS), order_index.reshape(1, DOCS))
    return result.reshape(DOCS)


def solution(mesh):
    placed = (P(("group", "member"), None), P(("group", "member")), P(("group", "member")))
    return jax.shard_map(
        local, mesh=mesh, in_specs=placed, out_specs=P(("group", "member")), check_vma=False
    )
```

time: 97.4 us -> 84.8 us (0.87)
  Pallas kernels: 94.9 us -> 82.4 us
    pallas_call x1, Pallas kernels: 94.9 us -> 82.4 us  [local(): pl.pallas_call(kernel, out_shape=jax.ShapeDtypeStruct((1, DOCS), jnp.floa...]
where the time goes in v2:
time: 84.8 us; the launch traced here: 84.7 us
  Pallas kernels  82.4 us (97%)
  local copies, waits for them, and re-layouts  2.32 us (3%)
    pallas_call x1, Pallas kernels, local(): pl.pallas_call(kernel, out_shape=jax.ShapeDtypeStruct((1, DOCS), jnp.floa...  82.4 us
    unnamed x7, local copies, waits for them, and re-layouts  2.32 us

profile of v2, /device:TPU:1, one launch (start us, length us, event | category | flops | bytes accessed | tf_op | source)
XLA Modules:
  0.0 84.7 jit_solution(14851791454434405705)
XLA Ops:
  0.0 0.0 copy-start.1
  0.0 0.0 copy-start.2
  0.0 0.7 copy-done.1
  0.7 0.0 copy-done.2
  0.7 0.0 copy-start
  0.7 1.1 %copy-done = bf16[96,4096]{1,0:T(8,128)(2,1)S(1)} copy-done((bf16[96,4096]{1,0:T(8,128)(2,1)S(1)}, bf16[96,4096]{1,0:T(8,128)(2,1)}, u32[]{:S(2)}) %copy-start) | copy-done | bytes 786456
  1.8 82.4 %shard_map.37 = f32[1,96]{1,0:T(1,128)S(1)} custom-call(bf16[96,4096]{1,0:T(8,128)(2,1)S(1)} %copy-done, s32[1,96]{1,0:T(1,128)S(1)} %bitcast.3, s32[1,96]{1,0:T(1,128)S(1)} %bitcast.4), custom_call_target="tpu_custom_call" | custom-call | tf_op jit(solution)/shard_map/pallas_call | solution.py:327
  84.2 0.5 copy.5
Async XLA Ops:
  0.0 0.7 copy-start.1
  0.0 0.7 copy-start.2
  0.7 1.1 %copy-start = (bf16[96,4096]{1,0:T(8,128)(2,1)S(1)}, bf16[96,4096]{1,0:T(8,128)(2,1)}, u32[]{:S(2)}) copy-start(bf16[96,4096]{1,0:T(8,128)(2,1)} %refs_0_.1) | copy-start | bytes 2359300

commit v3 on v2

--- a/solution.py
+++ b/solution.py
@@ -14,9 +14,13 @@
 SLOTS = NZ * CHUNK
 D = 4096
 META = 128
-WIDTHS = (512,) * 8
-STARTS = tuple(sum(WIDTHS[:p]) for p in range(len(WIDTHS)))
+W = META + D
+WIDTHS = (256,) + (512,) * 7 + (256,)
 PARTS = len(WIDTHS)
+STARTS = tuple(META + sum(WIDTHS[:p]) for p in range(PARTS))
+ENDS = tuple(s + w for s, w in zip(STARTS, WIDTHS))
+FAR = (4, 3, 5, 2, 6, 1, 7)
+REST = pl.ds(1, NZ - 1)
 
 OWN, XY, X1, X2, Y1, Y2 = range(6)
 BLOCKS = 6
@@ -31,12 +35,11 @@
 
 def kernel(*refs):
     emb_hbm, ids_hbm, ord_hbm, out_ref, emb, ids_ref, ord_ref = refs[:7]
-    downs, mrows, best, part, ans, fin, acc_own, acc_xy, units = refs[7:16]
-    outb = refs[16 : 16 + PARTS]
-    buf = refs[16 + PARTS : 16 + 2 * PARTS]
+    downs, mrows, best, part, total_ref, ans, acc_own, acc_xy, units, outb, buf = refs[7:18]
     (
         in_sem, sib_send, sib_recv, z_send, z_recv, send, recv, p_send, p_recv, a_send, a_recv,
-    ) = refs[16 + 2 * PARTS :]
+        near, far,
+    ) = refs[18:]
 
     gi = lax.axis_index("group")
     mi = lax.axis_index("member")
@@ -50,10 +53,10 @@
             mi,
         )
 
-    def at_z(step):
-        return (gi, lax.rem(z + step + NZ, NZ) * 2 + c)
-
-    sibling = (gi, z * 2 + 1 - c)
+    def at_z(step, core=c):
+        return (gi, lax.rem(z + step + NZ, NZ) * 2 + core)
+
+    sibling = at_z(0, 1 - c)
     back = {X1: at(-1, 0), Y1: at(0, -1), XY: at(-1, -1), X2: at(-2, 0), Y2: at(0, -2)}
 
     loads = [
@@ -64,8 +67,7 @@
     for load in loads:
         load.start()
 
-    peers = [sibling, at(1, 0), at(0, 1), at(1, 1), at(-1, 0), at(0, -1), at(-1, -1)]
-    peers += [at(2, 0), at(0, 2)] + [at_z(s) for s in range(1, NZ)]
+    peers = [sibling, at(1, 0), at(0, 1), at(-1, 0), at(0, -1), at_z(1), at_z(-1)]
     barrier = pltpu.get_barrier_semaphore()
     for peer in peers:
         pl.semaphore_signal(barrier, inc=1, device_id=peer, device_id_type=MESH)
@@ -112,6 +114,9 @@
 
     pl.semaphore_wait(barrier, len(peers))
 
+    for step in (1, -1):
+        pl.semaphore_signal(near, inc=1, device_id=at_z(step), device_id_type=MESH)
+
     sent = []
 
     def push(src, dst, ssem, rsem, device):
@@ -124,17 +129,9 @@
         return copy
 
     meta_copy = push(
-        mrows.at[0], mrows.at[1], sib_send.at[PARTS], sib_recv.at[PARTS], sibling
-    )
-    unit_copies = []
-    for p in range(PARTS):
-        columns = pl.ds(STARTS[p], WIDTHS[p])
-        unit_copies.append(
-            push(
-                units.at[0, :, columns], units.at[1, :, columns],
-                sib_send.at[p], sib_recv.at[p], sibling,
-            )
-        )
+        mrows.at[0], mrows.at[1], sib_send.at[1], sib_recv.at[1], sibling
+    )
+    unit_copy = push(units.at[0], units.at[1], sib_send.at[0], sib_recv.at[0], sibling)
 
     slot_iota = lax.broadcasted_iota(jnp.int32, (SLOTS, DOCS), 0).astype(jnp.float32)
 
@@ -152,31 +149,60 @@
     meta_copy.wait_recv()
     table_b, meta_b = table_of(1)
 
-    def place(p, values, start):
-        width = values.shape[-1]
-        values = values.reshape(NZ, CHUNK, width).astype(jnp.bfloat16)
-        buf[p][OWN, 0, :, start : start + width] = values[0]
-        outb[p][:, :, start : start + width] = values[1:]
+    pl.semaphore_wait(near, 2)
+    for step in (2, -2):
+        pl.semaphore_signal(far, inc=1, device_id=at_z(step), device_id_type=MESH)
+
+    copies = {}
+
+    def forward(src, dst, p, device):
+        if p < 0:
+            piece = lambda block: buf.at[block, 0]
+        else:
+            lo = 0 if p == 0 else STARTS[p]
+            columns = pl.ds(lo, ENDS[p] - lo)
+            piece = lambda block: buf.at[block, REST, :, columns]
+        copies[dst, p] = push(
+            piece(src), piece(dst), send.at[dst, p + 1], recv.at[dst, p + 1], device
+        )
+
+    unit_copy.wait_recv()
+    meta = (meta_a + meta_b).reshape(NZ, CHUNK, META).astype(jnp.bfloat16)
+    buf[OWN, 0, :, :META] = meta[0]
+    outb[:, :, :META] = meta[1:]
+    for p in range(PARTS):
+        columns = pl.ds(STARTS[p] - META, WIDTHS[p])
+        rows = jnp.dot(
+            table_a[:CHUNK], units[0, :, columns], preferred_element_type=jnp.float32
+        )
+        rows += jnp.dot(
+            table_b[:CHUNK], units[1, :, columns], preferred_element_type=jnp.float32
+        )
+        buf[OWN, 0, :, STARTS[p] : ENDS[p]] = rows.astype(jnp.bfloat16)
+    forward(OWN, X1, -1, at(1, 0))
+    forward(OWN, Y1, -1, at(0, 1))
 
     z_copies = {}
-    place(0, meta_a + meta_b, WIDTHS[0])
     for p in range(PARTS):
-        unit_copies[p].wait_recv()
-        columns = pl.ds(STARTS[p], WIDTHS[p])
-        rows = jnp.dot(table_a, units[0, :, columns], preferred_element_type=jnp.float32)
-        rows += jnp.dot(table_b, units[1, :, columns], preferred_element_type=jnp.float32)
-        place(p, rows, 0)
-        for k in (1, 7, 2, 6, 3, 5, 4):
+        columns = pl.ds(STARTS[p] - META, WIDTHS[p])
+        rows = jnp.dot(
+            table_a[CHUNK:], units[0, :, columns], preferred_element_type=jnp.float32
+        )
+        rows += jnp.dot(
+            table_b[CHUNK:], units[1, :, columns], preferred_element_type=jnp.float32
+        )
+        outb[:, :, STARTS[p] : ENDS[p]] = rows.reshape(NZ - 1, CHUNK, WIDTHS[p]).astype(
+            jnp.bfloat16
+        )
+        if p == 0:
+            pl.semaphore_wait(far, 2)
+        lo = 0 if p == 0 else STARTS[p]
+        columns = pl.ds(lo, ENDS[p] - lo)
+        for k in FAR:
             z_copies[p, k] = push(
-                outb[p].at[k - 1], buf[p].at[OWN, k], z_send.at[p, k], z_recv.at[p, k], at_z(k)
+                outb.at[k - 1, :, columns], buf.at[OWN, k, :, columns],
+                z_send.at[p, k], z_recv.at[p, k], at_z(k),
             )
-
-    copies = {}
-
-    def forward(src, dst, p, device):
-        copies[dst, p] = push(
-            buf[p].at[src], buf[p].at[dst], send.at[dst, p], recv.at[dst, p], device
-        )
 
     done = set()
 
@@ -198,14 +224,18 @@
     def multiply(p):
         for block in (XY, X2, Y2):
             arrived(block, p)
-        w = WIDTHS[p]
-        rows = buf[p][OWN, :, :, :w].reshape(SLOTS, w)
+        columns = pl.ds(STARTS[p], WIDTHS[p])
+
+        def rows_of(block):
+            return buf[block, :, :, columns].reshape(SLOTS, WIDTHS[p])
+
+        rows = rows_of(OWN)
         for block in range(BLOCKS):
-            acc_own[block] += nt_dot(buf[p][block, :, :, :w].reshape(SLOTS, w), rows)
+            acc_own[block] += nt_dot(rows_of(block), rows)
         for b in range(2):
-            columns = buf[p][Y1 + b, :, :, :w].reshape(SLOTS, w)
+            rows = rows_of(Y1 + b)
             for a in range(2):
-                acc_xy[a, b] += nt_dot(buf[p][X1 + a, :, :, :w].reshape(SLOTS, w), columns)
+                acc_xy[a, b] += nt_dot(rows_of(X1 + a), rows)
 
     pick_row = lax.broadcasted_iota(jnp.int32, (8, META), 0)
     pick_lane = lax.broadcasted_iota(jnp.int32, (8, META), 1)
@@ -214,7 +244,7 @@
     pick = jnp.where((pick_row == 1) & (pick_lane == 2), 1.0, pick).astype(jnp.bfloat16)
 
     def meta_of(block):
-        return buf[0][block, :, :, WIDTHS[0] :].reshape(SLOTS, META)
+        return buf[block, :, :, :META].reshape(SLOTS, META)
 
     def meta_down(block):
         values = meta_of(block).astype(jnp.float32)
@@ -226,6 +256,7 @@
 
     def start_sums():
         for block in (XY, X2, Y2):
+            arrived(block, -1)
             arrived(block, 0)
         across = {b: meta_across(b)[0] for b in (OWN, Y1, Y2)}
         for block in range(BLOCKS):
@@ -237,12 +268,11 @@
         downs[...] = jnp.full(downs.shape, -1.0, jnp.float32)
 
     for p in range(PARTS):
-        for k in (1, 7, 2, 6, 3, 5, 4):
+        for k in FAR:
             z_copies[p, k].wait_recv()
         forward(OWN, X1, p, at(1, 0))
         forward(OWN, Y1, p, at(0, 1))
-        if p >= 1:
-            relay(p - 1)
+        relay(p - 1)
         if p == 2:
             start_sums()
         if p >= 2:
@@ -293,29 +323,27 @@
         p_copies[n].wait_recv()
         total = jnp.maximum(total, part[n])
     total = jnp.max(total, axis=0, keepdims=True)
-    ans[0] = jnp.broadcast_to(total, (8, 256))
+    total_ref[...] = jnp.broadcast_to(total, (8, 256))
     a_copies = []
-    for k in range(1, NZ):
-        a_copies.append(push(ans.at[0], ans.at[k], a_send.at[k], a_recv.at[k], at_z(-k)))
+    for k in (4, 3, 5, 2, 6, 1, 7, 0):
+        for n, to in ((k, c), (NZ + k, 1 - c)):
+            if n:
+                a_copies.append(
+                    push(total_ref, ans.at[n], a_send.at[n], a_recv.at[n], at_z(-k, to))
+                )
+    ans[0] = total_ref[...]
+    spot = lax.broadcasted_iota(jnp.int32, (SLOTS, DOCS), 0) == slot
+    line = 8 * (offset + jnp.where(core == c, 0, NZ))
+    here = lax.broadcasted_iota(jnp.int32, (2 * NZ * 8, DOCS), 0) == line
     for copy in a_copies:
         copy.wait_recv()
-    fin[0] = jnp.zeros((8, 128), jnp.float32)
-    for k in range(NZ):
-        fin[0, k : k + 1, :CHUNK] = ans[k, 0:1, k * CHUNK : (k + 1) * CHUNK]
-    fin_copy = push(
-        fin.at[0], fin.at[1], sib_send.at[PARTS + 1], sib_recv.at[PARTS + 1], sibling
-    )
-    spot = (lax.broadcasted_iota(jnp.int32, (128, DOCS), 0) == inner).astype(jnp.float32)
-    offs = lax.broadcasted_iota(jnp.int32, (8, DOCS), 0) == offset
-    fin_copy.wait_recv()
-    picked = jnp.zeros((8, DOCS), jnp.float32)
-    for n in range(2):
-        values = jnp.dot(
-            fin[n], spot, preferred_element_type=jnp.float32, precision=lax.Precision.HIGHEST
-        )
-        at_core = jnp.where(core == (c if n == 0 else 1 - c), 1, 0)
-        picked += jnp.where(offs & (at_core == 1), values, 0.0)
-    out_ref[...] = jnp.sum(picked, axis=0, keepdims=True)
+    values = jnp.dot(
+        ans[:, :, :SLOTS].reshape(2 * NZ * 8, SLOTS),
+        spot.astype(jnp.float32),
+        preferred_element_type=jnp.float32,
+        precision=lax.Precision.HIGHEST,
+    )
+    out_ref[...] = jnp.sum(jnp.where(here, values, 0.0), axis=0, keepdims=True)
     for copy in sent:
         copy.wait_send()
 
@@ -323,11 +351,10 @@
 def local(embeddings, cluster_ids, order_index):
     dma = pltpu.SemaphoreType.DMA
     f32, bf16 = jnp.float32, jnp.bfloat16
-    widths = [w + (META if p == 0 else 0) for p, w in enumerate(WIDTHS)]
     result = pl.pallas_call(
         kernel,
         out_shape=jax.ShapeDtypeStruct((1, DOCS), jnp.float32),
-        in_specs=[pl.BlockSpec(memory_space=pltpu.HBM)] * 3,
+        in_specs=[pl.BlockSpec(memory_space=pl.ANY)] * 3,
         out_specs=pl.BlockSpec(memory_space=pltpu.VMEM),
         scratch_shapes=[
             pltpu.VMEM((DOCS, D), bf16),
@@ -337,29 +364,29 @@
             pltpu.VMEM((2, 8, 128), f32),
             pltpu.VMEM((BLOCKS, 8, 256), f32),
             pltpu.VMEM((len(RETURNS), 8, 256), f32),
-            pltpu.VMEM((NZ, 8, 256), f32),
-            pltpu.VMEM((2, 8, 128), f32),
+            pltpu.VMEM((8, 256), f32),
+            pltpu.VMEM((2 * NZ, 8, 256), f32),
             pltpu.VMEM((BLOCKS, SLOTS, SLOTS), f32),
             pltpu.VMEM((2, 2, SLOTS, SLOTS), f32),
             pltpu.VMEM((2, DOCS, D), bf16),
-        ]
-        + [pltpu.VMEM((NZ - 1, CHUNK, w), bf16) for w in widths]
-        + [pltpu.VMEM((BLOCKS, NZ, CHUNK, w), bf16) for w in widths]
-        + [
+            pltpu.VMEM((NZ - 1, CHUNK, W), bf16),
+            pltpu.VMEM((BLOCKS, NZ, CHUNK, W), bf16),
             dma((3,)),
-            dma((PARTS + 2,)),
-            dma((PARTS + 2,)),
+            dma((2,)),
+            dma((2,)),
             dma((PARTS, NZ)),
             dma((PARTS, NZ)),
-            dma((BLOCKS, PARTS)),
-            dma((BLOCKS, PARTS)),
+            dma((BLOCKS, PARTS + 1)),
+            dma((BLOCKS, PARTS + 1)),
             dma((len(RETURNS),)),
             dma((len(RETURNS),)),
-            dma((NZ,)),
-            dma((NZ,)),
+            dma((2 * NZ,)),
+            dma((2 * NZ,)),
+            pltpu.SemaphoreType.REGULAR,
+            pltpu.SemaphoreType.REGULAR,
         ],
         compiler_params=pltpu.CompilerParams(
-            collective_id=0, has_side_effects=True, vmem_limit_bytes=48 * 1024 * 1024
+            collective_id=0, has_side_effects=True, vmem_limit_bytes=67043328 - 384 * 1024
         ),
     )(embeddings, cluster_ids.reshape(1, DOCS), order_index.reshape(1, DOCS))
     return result.reshape(DOCS)

time: 84.8 us -> 79.8 us (0.941)
  Pallas kernels: 82.4 us -> 78.6 us
  local copies, waits for them, and re-layouts: 2.32 us -> 1.1 us
    pallas_call x1, Pallas kernels: 82.4 us -> 78.6 us  [local(): pl.pallas_call(kernel, out_shape=jax.ShapeDtypeStruct((1, DOCS), jnp.floa...]
    unnamed x7 -> x3, local copies, waits for them, and re-layouts: 2.32 us -> 1.1 us
where the time goes in v3:
time: 79.8 us; the launch traced here: 79.7 us
  Pallas kernels  78.6 us (98%)
  local copies, waits for them, and re-layouts  1.1 us (1%)
    pallas_call x1, Pallas kernels, local(): pl.pallas_call(kernel, out_shape=jax.ShapeDtypeStruct((1, DOCS), jnp.floa...  78.6 us

profile of v3, /device:TPU:1, one launch (start us, length us, event | category | flops | bytes accessed | tf_op | source)
XLA Modules:
  0.0 79.7 jit_solution(3369577666945723704)
XLA Ops:
  0.0 78.6 %shard_map.37 = f32[1,96]{1,0:T(1,128)} custom-call(bf16[96,4096]{1,0:T(8,128)(2,1)} %refs_0_.1, s32[1,96]{1,0:T(1,128)} %bitcast.3, s32[1,96]{1,0:T(1,128)} %bitcast.4), custom_call_target="tpu_custom_call" | custom-call | tf_op jit(solution)/shard_map/pallas_call | solution.py:354
  78.6 0.0 copy-start
  78.6 0.6 copy-done
  79.2 0.5 copy.5
Async XLA Ops:
  78.6 0.6 copy-start

commit v4 on v3

--- a/solution.py
+++ b/solution.py
@@ -15,16 +15,19 @@
 D = 4096
 META = 128
 W = META + D
-WIDTHS = (256,) + (512,) * 7 + (256,)
+WIDTHS = (256,)+(512,) * 7 + (256,)
 PARTS = len(WIDTHS)
 STARTS = tuple(META + sum(WIDTHS[:p]) for p in range(PARTS))
 ENDS = tuple(s + w for s, w in zip(STARTS, WIDTHS))
-FAR = (4, 3, 5, 2, 6, 1, 7)
-REST = pl.ds(1, NZ - 1)
+OFFSETS = (0, 1, 7, 2, 3, 4, 5, 6)
+NEAR = 1
+AHEAD = 3
+FAR = (5, 4, 6, 3, 7, 1, 2)
+REST = pl.ds(NEAR, NZ - NEAR)
 
 OWN, XY, X1, X2, Y1, Y2 = range(6)
 BLOCKS = 6
-RETURNS = (X1, Y1, XY, X2, Y2)
+RETURNS = (X2, Y2, XY, X1, Y1)
 
 
 def nt_dot(a, b):
@@ -55,6 +58,13 @@
 
     def at_z(step, core=c):
         return (gi, lax.rem(z + step + NZ, NZ) * 2 + core)
+
+    def bounds(p):
+        return (0 if p == 0 else STARTS[p]), ENDS[p]
+
+    def span(p):
+        first, last = bounds(p)
+        return pl.ds(first, last - first)
 
     sibling = at_z(0, 1 - c)
     back = {X1: at(-1, 0), Y1: at(0, -1), XY: at(-1, -1), X2: at(-2, 0), Y2: at(0, -2)}
@@ -89,7 +99,8 @@
     offset = lax.rem(target // 2 - z + NZ, NZ)
     core = lax.rem(target, 2)
     inner = c * CAP + rank
-    slot = offset * CHUNK + inner
+    place = jnp.where(offset <= 1, offset, jnp.where(offset == 7, 2, offset + 1))
+    slot = place * CHUNK + inner
     to_core0 = jnp.where(core == 0, slot, -1).astype(jnp.float32)
     to_core1 = jnp.where(core == 1, slot, -1).astype(jnp.float32)
     high = order // 256
@@ -103,15 +114,6 @@
     mrows[0, :, :DOCS] = packed
     mrows[0, :, DOCS:] = jnp.zeros((8, 128 - DOCS), jnp.float32)
 
-    loads[2].wait()
-
-    @pl.loop(0, DOCS // 16)
-    def _(i):
-        rows = pl.ds(pl.multiple_of(i * 16, 16), 16)
-        values = emb[rows, :].astype(jnp.float32)
-        total = jnp.sum(values * values, axis=1, keepdims=True) + D * 1e-06
-        units[0, rows, :] = (values * lax.rsqrt(total)).astype(jnp.bfloat16)
-
     pl.semaphore_wait(barrier, len(peers))
 
     for step in (1, -1):
@@ -128,10 +130,26 @@
         sent.append(copy)
         return copy
 
-    meta_copy = push(
-        mrows.at[0], mrows.at[1], sib_send.at[1], sib_recv.at[1], sibling
-    )
-    unit_copy = push(units.at[0], units.at[1], sib_send.at[0], sib_recv.at[0], sibling)
+    meta_copy = push(mrows.at[0], mrows.at[1], sib_send.at[2], sib_recv.at[2], sibling)
+
+    loads[2].wait()
+    unit_copies = []
+    for half in range(2):
+
+        @pl.loop(half * 3, half * 3 + 3)
+        def _(i):
+            rows = pl.ds(pl.multiple_of(i * 16, 16), 16)
+            values = emb[rows, :].astype(jnp.float32)
+            total = jnp.sum(values * values, axis=1, keepdims=True) + D * 1e-06
+            units[0, rows, :] = (values * lax.rsqrt(total)).astype(jnp.bfloat16)
+
+        rows = pl.ds(half * 48, 48)
+        unit_copies.append(
+            push(
+                units.at[0, rows], units.at[1, rows],
+                sib_send.at[half], sib_recv.at[half], sibling,
+            )
+        )
 
     slot_iota = lax.broadcasted_iota(jnp.int32, (SLOTS, DOCS), 0).astype(jnp.float32)
 
@@ -155,75 +173,82 @@
 
     copies = {}
 
-    def forward(src, dst, p, device):
-        if p < 0:
-            piece = lambda block: buf.at[block, 0]
+    def forward(src, dst, q, device, half=None):
+        first, last = (0, W) if q < NEAR else bounds(q - NEAR)
+        middle = first + (last - first) // 256 * 128
+        if half is not None:
+            first, last = ((first, middle), (middle, last))[half]
+        chunks = pl.ds(q, 1) if q < NEAR else REST
+        piece = lambda block: buf.at[block, chunks, :, pl.ds(first, last - first)]
+        slot = (dst, q) if half != 1 else (BLOCKS, q)
+        copies[(dst, q, half)] = push(
+            piece(src), piece(dst), send.at[slot], recv.at[slot], device
+        )
+
+    def pass_on(q):
+        forward(OWN, X1, q, at(1, 0))
+        forward(OWN, Y1, q, at(0, 1))
+
+    done = set()
+
+    def arrived(block, q):
+        if (block, q) not in done:
+            done.add((block, q))
+            for half in (0, 1) if block == XY else (None,):
+                copies[(block, q, half)].wait_recv()
+
+    def relay(q):
+        arrived(X1, q)
+        forward(X1, X2, q, at(1, 0))
+        forward(X1, XY, q, at(0, 1), 0)
+        arrived(Y1, q)
+        forward(Y1, Y2, q, at(0, 1))
+        forward(Y1, XY, q, at(1, 0), 1)
+
+    def build(first, last, start, end):
+        columns = pl.ds(start - META, end - start)
+        rows = jnp.dot(
+            table_a[first * CHUNK : last * CHUNK], units[0, :, columns],
+            preferred_element_type=jnp.float32,
+        )
+        rows += jnp.dot(
+            table_b[first * CHUNK : last * CHUNK], units[1, :, columns],
+            preferred_element_type=jnp.float32,
+        )
+        rows = rows.reshape(last - first, CHUNK, end - start).astype(jnp.bfloat16)
+        if first:
+            outb[first - 1 : last - 1, :, start:end] = rows
         else:
-            lo = 0 if p == 0 else STARTS[p]
-            columns = pl.ds(lo, ENDS[p] - lo)
-            piece = lambda block: buf.at[block, REST, :, columns]
-        copies[dst, p] = push(
-            piece(src), piece(dst), send.at[dst, p + 1], recv.at[dst, p + 1], device
-        )
-
-    unit_copy.wait_recv()
+            buf[OWN, 0, :, start:end] = rows[0]
+
+    for copy in unit_copies:
+        copy.wait_recv()
     meta = (meta_a + meta_b).reshape(NZ, CHUNK, META).astype(jnp.bfloat16)
     buf[OWN, 0, :, :META] = meta[0]
     outb[:, :, :META] = meta[1:]
+    for start in range(META, W, 1024):
+        build(0, 1, start, start + 1024)
+    pass_on(0)
+    z_copies = {}
+    def send_far(p):
+        if p < PARTS:
+            columns = span(p)
+            for k in FAR:
+                z_copies[p, k] = push(
+                    outb.at[k - 1, :, columns], buf.at[OWN, k, :, columns],
+                    z_send.at[p, k], z_recv.at[p, k], at_z(OFFSETS[k]),
+                )
+
     for p in range(PARTS):
-        columns = pl.ds(STARTS[p] - META, WIDTHS[p])
-        rows = jnp.dot(
-            table_a[:CHUNK], units[0, :, columns], preferred_element_type=jnp.float32
-        )
-        rows += jnp.dot(
-            table_b[:CHUNK], units[1, :, columns], preferred_element_type=jnp.float32
-        )
-        buf[OWN, 0, :, STARTS[p] : ENDS[p]] = rows.astype(jnp.bfloat16)
-    forward(OWN, X1, -1, at(1, 0))
-    forward(OWN, Y1, -1, at(0, 1))
-
-    z_copies = {}
-    for p in range(PARTS):
-        columns = pl.ds(STARTS[p] - META, WIDTHS[p])
-        rows = jnp.dot(
-            table_a[CHUNK:], units[0, :, columns], preferred_element_type=jnp.float32
-        )
-        rows += jnp.dot(
-            table_b[CHUNK:], units[1, :, columns], preferred_element_type=jnp.float32
-        )
-        outb[:, :, STARTS[p] : ENDS[p]] = rows.reshape(NZ - 1, CHUNK, WIDTHS[p]).astype(
-            jnp.bfloat16
-        )
+        build(NEAR, NZ, STARTS[p], ENDS[p])
         if p == 0:
             pl.semaphore_wait(far, 2)
-        lo = 0 if p == 0 else STARTS[p]
-        columns = pl.ds(lo, ENDS[p] - lo)
-        for k in FAR:
-            z_copies[p, k] = push(
-                outb.at[k - 1, :, columns], buf.at[OWN, k, :, columns],
-                z_send.at[p, k], z_recv.at[p, k], at_z(k),
-            )
-
-    done = set()
-
-    def arrived(block, p):
-        if (block, p) not in done:
-            done.add((block, p))
-            copies[block, p].wait_recv()
-
-    def relay(p):
-        arrived(X1, p)
-        forward(X1, X2, p, at(1, 0))
-        if p % 2 == 0:
-            forward(X1, XY, p, at(0, 1))
-        arrived(Y1, p)
-        forward(Y1, Y2, p, at(0, 1))
-        if p % 2 == 1:
-            forward(Y1, XY, p, at(1, 0))
+        if p < AHEAD:
+            send_far(p)
 
     def multiply(p):
         for block in (XY, X2, Y2):
-            arrived(block, p)
+            arrived(block, p + NEAR)
         columns = pl.ds(STARTS[p], WIDTHS[p])
 
         def rows_of(block):
@@ -256,8 +281,8 @@
 
     def start_sums():
         for block in (XY, X2, Y2):
-            arrived(block, -1)
-            arrived(block, 0)
+            for q in range(NEAR + 1):
+                arrived(block, q)
         across = {b: meta_across(b)[0] for b in (OWN, Y1, Y2)}
         for block in range(BLOCKS):
             down = meta_down(block)[0]
@@ -267,17 +292,19 @@
                     acc_xy[block - X1, b] = jnp.where(down == across[Y1 + b], 0.0, -4.0)
         downs[...] = jnp.full(downs.shape, -1.0, jnp.float32)
 
+    relay(0)
     for p in range(PARTS):
         for k in FAR:
             z_copies[p, k].wait_recv()
-        forward(OWN, X1, p, at(1, 0))
-        forward(OWN, Y1, p, at(0, 1))
-        relay(p - 1)
+        send_far(p + AHEAD)
+        pass_on(p + NEAR)
+        if p:
+            relay(p)
         if p == 2:
             start_sums()
         if p >= 2:
             multiply(p - 2)
-    relay(PARTS - 1)
+    relay(PARTS + NEAR - 1)
     multiply(PARTS - 2)
     multiply(PARTS - 1)
 
@@ -302,43 +329,40 @@
             merge(rows, X1 + a, over_columns(sums, down[X1 + a], across[Y1 + b]))
             if (a, b) != (1, 1):
                 merge(lanes, Y1 + b, over_rows(sums, down[X1 + a], across[Y1 + b]))
-    for block in range(BLOCKS):
-        sums = acc_own[block]
-        merge(lanes, OWN, over_rows(sums, down[block], across[OWN]))
-        if block in (XY, X1, Y1):
-            merge(rows, block, over_columns(sums, down[block], across[OWN]))
-    for n, block in enumerate((XY, X1, X2, Y1)):
-        downs[n, :, :SLOTS] = rows[block]
-        narrow = jnp.maximum(downs[n, :, :128], downs[n, :, 128:])
-        turned = jnp.max(narrow.T, axis=0, keepdims=True)
-        merge(lanes, block, jnp.broadcast_to(turned, (8, SLOTS)))
-    for block in range(BLOCKS):
-        best[block, :, :SLOTS] = lanes[block]
-
+    for block in (XY, X1, Y1):
+        merge(rows, block, over_columns(acc_own[block], down[block], across[OWN]))
     p_copies = []
     for n, block in enumerate(RETURNS):
+        if block in rows and rows[block] is not None:
+            downs[n, :, :SLOTS] = rows[block]
+            narrow = jnp.maximum(downs[n, :, :128], downs[n, :, 128:])
+            turned = jnp.max(narrow.T, axis=0, keepdims=True)
+            merge(lanes, block, jnp.broadcast_to(turned, (8, SLOTS)))
+        best[block, :, :SLOTS] = jnp.max(lanes[block], axis=0, keepdims=True)
         p_copies.append(push(best.at[block], part.at[n], p_send.at[n], p_recv.at[n], back[block]))
+    for block in range(BLOCKS):
+        merge(lanes, OWN, over_rows(acc_own[block], down[block], across[OWN]))
+    best[OWN, :, :SLOTS] = jnp.max(lanes[OWN], axis=0, keepdims=True)
     total = best[OWN]
     for n in range(len(RETURNS)):
         p_copies[n].wait_recv()
         total = jnp.maximum(total, part[n])
-    total = jnp.max(total, axis=0, keepdims=True)
-    total_ref[...] = jnp.broadcast_to(total, (8, 256))
+    total_ref[...] = total
     a_copies = []
-    for k in (4, 3, 5, 2, 6, 1, 7, 0):
+    for k in FAR + (0,):
         for n, to in ((k, c), (NZ + k, 1 - c)):
             if n:
                 a_copies.append(
-                    push(total_ref, ans.at[n], a_send.at[n], a_recv.at[n], at_z(-k, to))
+                    push(total_ref, ans.at[n], a_send.at[n], a_recv.at[n], at_z(-OFFSETS[k], to))
                 )
     ans[0] = total_ref[...]
     spot = lax.broadcasted_iota(jnp.int32, (SLOTS, DOCS), 0) == slot
-    line = 8 * (offset + jnp.where(core == c, 0, NZ))
-    here = lax.broadcasted_iota(jnp.int32, (2 * NZ * 8, DOCS), 0) == line
+    line = place + jnp.where(core == c, 0, NZ)
+    here = lax.broadcasted_iota(jnp.int32, (2 * NZ, DOCS), 0) == line
     for copy in a_copies:
         copy.wait_recv()
     values = jnp.dot(
-        ans[:, :, :SLOTS].reshape(2 * NZ * 8, SLOTS),
+        ans[:, :, :SLOTS].reshape(2 * NZ, SLOTS),
         spot.astype(jnp.float32),
         preferred_element_type=jnp.float32,
         precision=lax.Precision.HIGHEST,
@@ -360,24 +384,24 @@
             pltpu.VMEM((DOCS, D), bf16),
             pltpu.VMEM((1, DOCS), jnp.int32),
             pltpu.VMEM((1, DOCS), jnp.int32),
-            pltpu.VMEM((4, SLOTS, 256), f32),
+            pltpu.VMEM((len(RETURNS), SLOTS, 256), f32),
             pltpu.VMEM((2, 8, 128), f32),
-            pltpu.VMEM((BLOCKS, 8, 256), f32),
-            pltpu.VMEM((len(RETURNS), 8, 256), f32),
-            pltpu.VMEM((8, 256), f32),
-            pltpu.VMEM((2 * NZ, 8, 256), f32),
+            pltpu.VMEM((BLOCKS, 1, 256), f32),
+            pltpu.VMEM((len(RETURNS), 1, 256), f32),
+            pltpu.VMEM((1, 256), f32),
+            pltpu.VMEM((2 * NZ, 1, 256), f32),
             pltpu.VMEM((BLOCKS, SLOTS, SLOTS), f32),
             pltpu.VMEM((2, 2, SLOTS, SLOTS), f32),
             pltpu.VMEM((2, DOCS, D), bf16),
             pltpu.VMEM((NZ - 1, CHUNK, W), bf16),
             pltpu.VMEM((BLOCKS, NZ, CHUNK, W), bf16),
             dma((3,)),
-            dma((2,)),
-            dma((2,)),
-            dma((PARTS, NZ)),
-            dma((PARTS, NZ)),
-            dma((BLOCKS, PARTS + 1)),
-            dma((BLOCKS, PARTS + 1)),
+            dma((3,)),
+            dma((3,)),
+            dma((PARTS + 1, NZ)),
+            dma((PARTS + 1, NZ)),
+            dma((BLOCKS + 1, PARTS + NEAR)),
+            dma((BLOCKS + 1, PARTS + NEAR)),
             dma((len(RETURNS),)),
             dma((len(RETURNS),)),
             dma((2 * NZ,)),

time: 79.8 us -> 77.4 us (0.970)
  Pallas kernels: 78.6 us -> 76.2 us
    pallas_call x1, Pallas kernels: 78.6 us -> 76.2 us  [local(): pl.pallas_call(kernel, out_shape=jax.ShapeDtypeStruct((1, DOCS), jnp.floa...]
where the time goes in v4:
time: 77.4 us; the launch traced here: 77.3 us
  Pallas kernels  76.2 us (98%)
  local copies, waits for them, and re-layouts  1.1 us (1%)
    pallas_call x1, Pallas kernels, local(): pl.pallas_call(kernel, out_shape=jax.ShapeDtypeStruct((1, DOCS), jnp.floa...  76.2 us

profile of v4, /device:TPU:1, one launch (start us, length us, event | category | flops | bytes accessed | tf_op | source)
XLA Modules:
  0.0 77.3 jit_solution(240950739847458435)
XLA Ops:
  0.0 76.2 %shard_map.37 = f32[1,96]{1,0:T(1,128)} custom-call(bf16[96,4096]{1,0:T(8,128)(2,1)} %refs_0_.1, s32[1,96]{1,0:T(1,128)} %bitcast.3, s32[1,96]{1,0:T(1,128)} %bitcast.4), custom_call_target="tpu_custom_call" | custom-call | tf_op jit(solution)/shard_map/pallas_call | solution.py:378
  76.2 0.0 copy-start
  76.2 0.6 copy-done
  76.8 0.5 copy.5
Async XLA Ops:
  76.2 0.6 copy-start

commit v5 on v4

--- a/solution.py
+++ b/solution.py
@@ -22,6 +22,7 @@
 OFFSETS = (0, 1, 7, 2, 3, 4, 5, 6)
 NEAR = 1
 AHEAD = 3
+LAG = 3
 FAR = (5, 4, 6, 3, 7, 1, 2)
 REST = pl.ds(NEAR, NZ - NEAR)
 
@@ -296,17 +297,17 @@
     for p in range(PARTS):
         for k in FAR:
             z_copies[p, k].wait_recv()
-        send_far(p + AHEAD)
         pass_on(p + NEAR)
         if p:
             relay(p)
-        if p == 2:
+        send_far(p + AHEAD)
+        if p == LAG:
             start_sums()
-        if p >= 2:
-            multiply(p - 2)
+        if p >= LAG:
+            multiply(p - LAG)
     relay(PARTS + NEAR - 1)
-    multiply(PARTS - 2)
-    multiply(PARTS - 1)
+    for p in range(PARTS - LAG, PARTS):
+        multiply(p)
 
     def over_rows(sums, down, across):
         kept = jnp.where(down < across, sums, -1.0)

time: 77.4 us -> 77.4 us (level)
  no operation moved by 1% of the time
where the time goes in v5:
time: 77.4 us; the launch traced here: 77.3 us
  Pallas kernels  76.2 us (98%)
  local copies, waits for them, and re-layouts  1.1 us (1%)
    pallas_call x1, Pallas kernels, local(): pl.pallas_call(kernel, out_shape=jax.ShapeDtypeStruct((1, DOCS), jnp.floa...  76.2 us

profile of v5, /device:TPU:1, one launch (start us, length us, event | category | flops | bytes accessed | tf_op | source)
XLA Modules:
  0.0 77.3 jit_solution(4652727958541829214)
XLA Ops:
  0.0 76.2 %shard_map.37 = f32[1,96]{1,0:T(1,128)} custom-call(bf16[96,4096]{1,0:T(8,128)(2,1)} %refs_0_.1, s32[1,96]{1,0:T(1,128)} %bitcast.3, s32[1,96]{1,0:T(1,128)} %bitcast.4), custom_call_target="tpu_custom_call" | custom-call | tf_op jit(solution)/shard_map/pallas_call | solution.py:379
  76.2 0.0 copy-start
  76.2 0.6 copy-done
  76.8 0.5 copy.5
Async XLA Ops:
  76.2 0.6 copy-start

commit v6 on v5

--- a/solution.py
+++ b/solution.py
@@ -15,7 +15,7 @@
 D = 4096
 META = 128
 W = META + D
-WIDTHS = (256,)+(512,) * 7 + (256,)
+WIDTHS = (128, 384) + (512,) * 7
 PARTS = len(WIDTHS)
 STARTS = tuple(META + sum(WIDTHS[:p]) for p in range(PARTS))
 ENDS = tuple(s + w for s, w in zip(STARTS, WIDTHS))

time: 77.4 us -> 77.5 us (level)
  no operation moved by 1% of the time
where the time goes in v6:
time: 77.5 us; the launch traced here: 77.4 us
  Pallas kernels  76.3 us (98%)
  local copies, waits for them, and re-layouts  1.1 us (1%)
    pallas_call x1, Pallas kernels, local(): pl.pallas_call(kernel, out_shape=jax.ShapeDtypeStruct((1, DOCS), jnp.floa...  76.3 us

profile of v6, /device:TPU:1, one launch (start us, length us, event | category | flops | bytes accessed | tf_op | source)
XLA Modules:
  0.0 77.4 jit_solution(15173717628204574744)
XLA Ops:
  0.0 76.3 %shard_map.37 = f32[1,96]{1,0:T(1,128)} custom-call(bf16[96,4096]{1,0:T(8,128)(2,1)} %refs_0_.1, s32[1,96]{1,0:T(1,128)} %bitcast.3, s32[1,96]{1,0:T(1,128)} %bitcast.4), custom_call_target="tpu_custom_call" | custom-call | tf_op jit(solution)/shard_map/pallas_call | solution.py:379
  76.3 0.0 copy-start
  76.3 0.6 copy-done
  76.9 0.5 copy.5
Async XLA Ops:
  76.3 0.6 copy-start
